TPU v7x, 32 devices: a whole 2x2x4 slice. The times are simulated.
32 devices in a mesh: group: 1, wide: 32 (over z, y, x, core).
Axes of the slice: x: 2, y: 2, z: 4, core: 2. Of those that a mesh axis runs over, the one named last changes fastest.
Arguments:
- ssd_x: bfloat16 [2048, 4096], P(('group', 'wide')), may hold values from -6 to 6
- ssd_z: bfloat16 [2048, 4096], P(('group', 'wide')), may hold values from -6 to 6
- ssd_b: bfloat16 [2048, 128], P(('group', 'wide')), may hold values from -2 to 2
- ssd_c: bfloat16 [2048, 128], P(('group', 'wide')), may hold values from -2 to 2
- dt_raw: bfloat16 [2048, 64], P(('group', 'wide')), may hold values from -4 to 4
- dt_bias: float32 [64], replicated, may hold values from -4 to -1
- a_log: float32 [64], replicated, may hold values from -1.5 to 1.5
- d_skip: float32 [64], replicated, may hold values from 0.5 to 1.5
- norm_gain: float32 [4096], replicated, may hold values from 0.1 to 1.9
- cache_state: bfloat16 [64, 64, 64, 128], P(('group', 'wide')), may hold values from -2 to 2
- cache_owner: int32 [64], P('group'), may hold values from 0 to 63
- resid: bfloat16 [2048, 2048], P(('group', 'wide')), may hold values from -3 to 3
- w_out: bfloat16 [4096, 2048], P('wide'), may hold values from -0.09375 to 0.09375
- moe_gain: float32 [2048], replicated, may hold values from 0.1 to 1.9
- expert_ids: int32 [2048, 10], P(('group', 'wide')), may hold values from 0 to 31, all different within a row; in each aligned block of 64 rows (0 to 63, 64 to 127, ...) at most 32 rows name the same one
- route_weight: int32 [2048, 10], P(('group', 'wide')), may hold values from 1 to 1023
- expert_home: int32 [32], replicated, may hold values from 0 to 31, each once
- w_gate: bfloat16 [32, 2048, 384], P('wide'), may hold values from -0.125 to 0.125
- w_up: bfloat16 [32, 2048, 384], P('wide'), may hold values from -0.125 to 0.125
- w_down: bfloat16 [32, 384, 2048], P('wide'), may hold values from -0.3125 to 0.3125
Outputs:
- ssd_out: bfloat16 [2048, 4096], P(('group', 'wide'))
- moe_out: bfloat16 [2048, 2048], P(('group', 'wide'))
Inputs may be any that keep to these rules, and one draw needn't show every extreme that they name: `cache_owner`: slot s of cache_state holds a cached prefix state; several requests may continue from the same slot. `expert_ids`: each token names 10 different experts. In each aligned block of 64 tokens (the tokens of one device) no expert is named by more than 32 tokens, and in every draw some expert is named by exactly 32 tokens of some block. `expert_home`: A permutation of the experts.
All inputs are finite; a program needn't handle non-finite values.
Results may differ from a plain program's by a relative error of at most 0.02.
Values may be sent and summed in bfloat16 or wider, within the bound.
No kernel may reach another device: no remote copies, remote signals or barrier semaphores. Data moves between devices by JAX's collectives and lax.ppermute only.
A program may use at most 128 MiB of HBM per device.

v0:
```python
import jax
import jax.numpy as jnp
from jax import lax
from jax.sharding import PartitionSpec as P

SEQ = 32


def intra_terms(inputs, step_size, cumulative, b_proj, c_proj, skip_gain):
    scores = jnp.einsum("rtn,rsn->rts", c_proj, b_proj, preferred_element_type=jnp.float32)
    length = inputs.shape[1]
    causal = jnp.arange(length)[:, None] >= jnp.arange(length)[None, :]
    cum_heads = jnp.swapaxes(cumulative, 1, 2)
    log_gap = cum_heads[..., :, None] - cum_heads[..., None, :]
    decays = jnp.where(causal, jnp.exp(jnp.where(causal, log_gap, 0.0)), 0.0)
    mixing = (scores[:, None] * decays * jnp.swapaxes(step_size, 1, 2)[:, :, None, :]).astype(
        jnp.bfloat16
    )
    result = jnp.einsum("rhts,rshp->rthp", mixing, inputs, preferred_element_type=jnp.float32)
    result = result + skip_gain[None, None, :, None] * inputs.astype(jnp.float32)
    return result.astype(jnp.bfloat16)


def state_terms(c_proj, cumulative, start_state):
    product = jnp.einsum("rtn,rhpn->rthp", c_proj, start_state, preferred_element_type=jnp.float32)
    return (product * jnp.exp(cumulative)[..., None]).astype(jnp.bfloat16)


def expert_mlp(row_set, gate_weight, up_weight, down_weight):
    gate_out = jnp.dot(row_set, gate_weight, preferred_element_type=jnp.float32)
    up_out = jnp.dot(row_set, up_weight, preferred_element_type=jnp.float32)
    hidden = (jax.nn.silu(gate_out) * up_out).astype(jnp.bfloat16)
    return jnp.dot(hidden, down_weight, preferred_element_type=jnp.float32).astype(jnp.bfloat16)


def head_steps(raw_steps, bias_part, rate_part, requests):
    step_size = jax.nn.softplus(raw_steps.astype(jnp.float32) + bias_part)
    step_size = step_size.reshape(requests, SEQ, step_size.shape[-1])
    return (step_size, jnp.cumsum(step_size * rate_part, axis=1))


def local(
    ssd_x,
    ssd_z,
    ssd_b,
    ssd_c,
    dt_raw,
    dt_bias,
    a_log,
    d_skip,
    norm_gain,
    cache_state,
    cache_owner,
    resid,
    w_out,
    moe_gain,
    expert_ids,
    route_weight,
    expert_home,
    w_gate,
    w_up,
    w_down,
):
    devices = lax.axis_size("wide")
    my_index = lax.axis_index("wide")
    tok_dev = ssd_x.shape[0]
    heads_all = dt_raw.shape[1]
    per_dev = heads_all // devices
    head_dim = ssd_x.shape[1] // heads_all
    state_size = ssd_b.shape[1]
    req_local = tok_dev // SEQ
    rates = -jnp.exp(a_log)
    bias_part = lax.dynamic_slice_in_dim(dt_bias, my_index * per_dev, per_dev)
    rate_part = lax.dynamic_slice_in_dim(rates, my_index * per_dev, per_dev)
    by_heads = lax.all_to_all(cache_state, "wide", split_axis=1, concat_axis=0, tiled=True)
    start_state = jnp.take(by_heads, cache_owner, axis=0)
    requests = cache_owner.shape[0]
    tokens_all = requests * SEQ
    local_step, local_cum = head_steps(dt_raw, dt_bias, rates, req_local)
    intra = intra_terms(
        ssd_x.reshape(req_local, SEQ, heads_all, head_dim),
        local_step,
        local_cum,
        ssd_b.reshape(req_local, SEQ, state_size),
        ssd_c.reshape(req_local, SEQ, state_size),
        d_skip,
    )
    intra = intra.reshape(tok_dev, heads_all * head_dim)
    c_all = lax.all_gather(ssd_c, "wide", axis=0, tiled=True)
    head_raw = lax.all_to_all(dt_raw, "wide", split_axis=1, concat_axis=0, tiled=True)
    step_size, cumulative = head_steps(head_raw, bias_part, rate_part, requests)
    carried_head = state_terms(c_all.reshape(requests, SEQ, state_size), cumulative, start_state)
    carried = lax.all_to_all(
        carried_head.reshape(tokens_all, per_dev * head_dim),
        "wide",
        split_axis=0,
        concat_axis=1,
        tiled=True,
    )
    mixed = intra.astype(jnp.float32) + carried.astype(jnp.float32)
    gated = mixed * jax.nn.silu(ssd_z.astype(jnp.float32))
    ssd_out = (
        gated * lax.rsqrt(jnp.mean(gated * gated, axis=-1, keepdims=True) + 1e-05) * norm_gain
    ).astype(jnp.bfloat16)
    width = resid.shape[1]
    projected = jnp.dot(
        ssd_out,
        lax.all_gather(w_out, "wide", axis=0, tiled=True),
        preferred_element_type=jnp.float32,
    )
    topk = expert_ids.shape[1]
    expert_count = expert_home.shape[0]
    wide_moe = resid.astype(jnp.float32) + projected
    normed = (
        wide_moe
        * lax.rsqrt(jnp.mean(wide_moe * wide_moe, axis=-1, keepdims=True) + 1e-05)
        * moe_gain
    ).astype(jnp.bfloat16)
    weight_f = route_weight.astype(jnp.float32)
    share = weight_f / jnp.sum(weight_f, axis=-1, keepdims=True)
    lookup = expert_ids[..., None] == jnp.arange(expert_count, dtype=jnp.int32)
    target = jnp.sum(jnp.where(lookup, expert_home, 0), axis=-1)
    pair_count = tok_dev * topk
    flat_target = target.reshape(pair_count)
    one_hot = (flat_target[:, None] == jnp.arange(devices, dtype=jnp.int32)).astype(jnp.int32)
    before = jnp.cumsum(one_hot, axis=0) - one_hot
    slot_of = jnp.sum(before * one_hot, axis=-1)
    capacity = tok_dev * topk // expert_count * 8 // 5
    position = flat_target * capacity + slot_of
    source_row = (
        jnp.zeros((devices * capacity,), jnp.int32)
        .at[position]
        .set(jnp.arange(pair_count, dtype=jnp.int32) // topk + 1)
    )
    filled = source_row > 0
    fetched = jnp.take(normed, jnp.maximum(source_row - 1, 0), axis=0)
    send_rows = jnp.where(filled[:, None], fetched, jnp.zeros((), jnp.bfloat16)).reshape(
        devices, capacity, width
    )
    received = lax.all_to_all(send_rows, "wide", split_axis=0, concat_axis=0, tiled=True)
    flat_rows = received.reshape(-1, received.shape[-1])
    outputs = expert_mlp(flat_rows, w_gate[0], w_up[0], w_down[0]).reshape(received.shape)
    returned = lax.all_to_all(outputs, "wide", split_axis=0, concat_axis=0, tiled=True)
    gathered = jnp.take(returned.reshape(devices * capacity, width), position, axis=0).reshape(
        tok_dev, topk, width
    )
    moe_out = jnp.sum(gathered.astype(jnp.float32) * share[..., None], axis=1).astype(jnp.bfloat16)
    return (ssd_out, moe_out)


def solution(mesh):
    in_specs = (
        P(("group", "wide"), None),
        P(("group", "wide"), None),
        P(("group", "wide"), None),
        P(("group", "wide"), None),
        P(("group", "wide"), None),
        P(),
        P(),
        P(),
        P(),
        P(("group", "wide"), None, None, None),
        P("group"),
        P(("group", "wide"), None),
        P("wide", None),
        P(),
        P(("group", "wide"), None),
        P(("group", "wide"), None),
        P(),
        P("wide", None, None),
        P("wide", None, None),
        P("wide", None, None),
    )
    out_specs = (P(("group", "wide"), None), P(("group", "wide"), None))
    return jax.shard_map(local, mesh=mesh, in_specs=in_specs, out_specs=out_specs, check_vma=False)
```

profile of v0, /device:TPU:0, one launch (start us, length us, event | category | flops | bytes accessed | tf_op | source)
XLA Modules:
  0.0 430.2 jit_solution(291242435058443857)
XLA Ops:
  9.3 7.3 %all-to-all-start.1 = ((bf16[64,32,2]{0,2,1:T(2,128)(2,1)}), bf16[64,32,2]{0,2,1:T(2,128)(2,1)S(1)}, u32[]{:S(2)}, u32[]{:S(2)}) async-start(bf16[64,32,2]{0,2,1:T(2,128)(2,1)} %bitcast.14), calls=%async_computation.1 | async-start | bytes 32768 | tf_op jit(solution)/shard_map/all_to_all | solution.py:90
  16.7 3.1 copy.105
  19.8 3.9 all-to-all-done.1
  23.8 3.5 all-to-all-start
  31.5 2.5 copy.104
  38.0 84.1 %all_gather.6 = bf16[2048,128]{1,0:T(8,128)(2,1)S(1)} all-gather(bf16[64,128]{1,0:T(8,128)(2,1)S(1)} %copy-done.6), channel_id=1, replica_groups=mesh['group'=1,'wide'=32] {'wide'}, dimensions={0}, use_global_device_ids=true | all-gather | bytes 540672 | tf_op jit(solution)/shard_map/all_gather | solution.py:89
  128.0 3.2 copy.107
  131.1 3.8 gather_fusion
  134.9 3.7 fusion
  140.7 3.2 all_to_all.45
  143.9 15.3 %all-to-all-start.2 = ((bf16[32,64,128]{2,1,0:T(8,128)(2,1)}), bf16[32,64,128]{2,1,0:T(8,128)(2,1)S(1)}, u32[]{:S(2)}, u32[]{:S(2)}) async-start(bf16[32,64,128]{2,1,0:T(8,128)(2,1)} %all_to_all.45), calls=%async_computation.2 | async-start | bytes 1048576 | tf_op jit(solution)/shard_map/all_to_all | solution.py:93
  159.6 4.1 scatter_custom_fusion
  163.9 10.9 %all-to-all-done.2 = bf16[32,64,128]{2,1,0:T(8,128)(2,1)S(1)} async-done(((bf16[32,64,128]{2,1,0:T(8,128)(2,1)}), bf16[32,64,128]{2,1,0:T(8,128)(2,1)S(1)}, u32[]{:S(2)}, u32[]{:S(2)}) %all-to-all-start.2) | async-done | bytes 524320 | tf_op jit(solution)/shard_map/all_to_all | solution.py:93
  176.6 9.1 %multiply_reduce_fusion.2 = (f32[64]{0:T(128)S(1)}, f32[64,2048]{1,0:T(8,128)S(1)}) fusion(bf16[64,4096]{1,0:T(8,128)(2,1)S(1)} %multiply_convert_fusion.3, bf16[4096,2048]{1,0:T(8,128)(2,1)} %all-gather.2.cloned.1.call-done, bf16[64,2048]{1,0:T(8,128)(2,1)S(1)} %copy-done.4), kind=kOutput, calls=%fused_computation.42 | convolution fusion | flops 1074266112 | bytes 18088192 | tf_op jit(solution)/shard_map/dot_general | solution.py:106
  185.8 6.0 %gather_fusion.1 = bf16[1024,2048]{1,0:T(8,128)(2,1)} fusion(bf16[64,2048]{1,0:T(8,128)(2,1)S(1)} %multiply_convert_fusion.4, s32[1024]{0:T(1024)S(1)} %fusion.38), kind=kCustom, calls=%fused_computation.1 | custom fusion | bytes 8392704 | tf_op jit(solution)/shard_map/jit(_take)/gather | solution.py:136
  191.8 2.6 select_select_fusion
  194.4 96.4 %all_to_all.54 = bf16[32,32,2048]{2,1,0:T(8,128)(2,1)S(1)} all-to-all(bf16[32,32,2048]{2,1,0:T(8,128)(2,1)S(1)} %select_select_fusion), channel_id=1, replica_groups=mesh['group'=1,'wide'=32] {'wide'}, dimensions={0} | all-to-all | bytes 8388608 | tf_op jit(solution)/shard_map/all_to_all | solution.py:140
  292.8 3.6 fusion.8
  296.4 7.8 %convolution_convert_fusion = bf16[1024,2048]{1,0:T(8,128)(2,1)} fusion(bf16[1,384,2048]{2,1,0:T(8,128)(2,1)S(1)} %copy-done, f32[1024,384]{1,0:T(8,128)} %fusion.8, bf16[1024,2048]{1,0:T(8,128)(2,1)} %bitcast.90, bf16[1,2048,384]{2,1,0:T(8,128)(2,1)S(1)} %copy-done.15), kind=kOutput, calls=%fused_computation.6 | convolution fusion | flops 3225681920 | bytes 13107200 | tf_op jit(solution)/shard_map/dot_general | solution.py:33
  304.1 4.0 all-to-all-start.4
  308.7 93.2 %all-to-all-done.4 = bf16[32,32,2048]{2,1,0:T(8,128)(2,1)} async-done(((bf16[32,32,2048]{2,1,0:T(8,128)(2,1)}), bf16[32,32,2048]{2,1,0:T(8,128)(2,1)}, u32[]{:S(2)}, u32[]{:S(2)}) %all-to-all-start.4) | async-done | bytes 4194336 | tf_op jit(solution)/shard_map/all_to_all | solution.py:143
  401.9 9.7 %gather_fusion.2 = bf16[640,2048]{1,0:T(8,128)(2,1)} fusion(bf16[1024,2048]{1,0:T(8,128)(2,1)} %bitcast.24, s32[1024]{0:T(1024)S(1)} %pad_clamp_fusion), kind=kCustom, calls=%fused_computation.2 | custom fusion | bytes 5245440 | tf_op jit(solution)/shard_map/jit(_take)/gather | solution.py:144
  411.5 5.4 %gather.20 = bf16[64,10,2048]{2,1,0:T(8,128)(2,1)} reshape(bf16[640,2048]{1,0:T(8,128)(2,1)} %gather_fusion.2) | data formatting | bytes 5242880 | tf_op jit(solution)/shard_map/jit(_take)/gather | solution.py:144
  416.9 6.4 %multiply_reduce_fusion = bf16[64,2048]{1,0:T(8,128)(2,1)} fusion(f32[64,10]{1,0:T(8,128)S(1)} %copy.121, bf16[64,10,2048]{2,1,0:T(8,128)(2,1)} %gather.20, pred[64,10]{1,0:T(8,128)(4,1)S(1)} %copy.119), kind=kLoop, calls=%fused_computation.4 | loop fusion | flops 5111808 | bytes 2886784 | tf_op jit(solution)/shard_map/reduce_sum | solution.py:147
  (99 shorter events, 23.0 us)
Async XLA Ops:
  7.2 289.2 %copy-start = (bf16[1,384,2048]{2,1,0:T(8,128)(2,1)S(1)}, bf16[1,384,2048]{2,1,0:T(8,128)(2,1)}, u32[]{:S(2)}) copy-start(bf16[1,384,2048]{2,1,0:T(8,128)(2,1)} %param.39) | copy-start | bytes 4718596
  7.2 169.4 %all-gather.2.cloned.1.call-start = ((), (), s32[]{:S(2)}) async-start(), calls=%async_computation.5 | async-start | bytes 17301504 | tf_op jit(solution)/shard_map/all_gather | solution.py:108
  9.3 14.4 %all-to-all-start.1 = ((bf16[64,32,2]{0,2,1:T(2,128)(2,1)}), bf16[64,32,2]{0,2,1:T(2,128)(2,1)S(1)}, u32[]{:S(2)}, u32[]{:S(2)}) async-start(bf16[64,32,2]{0,2,1:T(2,128)(2,1)} %bitcast.14), calls=%async_computation.1 | async-start | bytes 32768 | tf_op jit(solution)/shard_map/all_to_all | solution.py:90
  19.8 7.5 %copy-start.11 = (s32[64,10]{0,1:T(8,128)S(1)}, s32[64,10]{0,1:T(8,128)}, u32[]{:S(2)}) copy-start(s32[64,10]{0,1:T(8,128)} %param.34) | copy-start | bytes 7684
  19.8 7.5 %copy-start.13 = (s32[32]{0:T(128)S(1)}, s32[32]{0:T(128)}, u32[]{:S(2)}) copy-start(s32[32]{0:T(128)} %param.36) | copy-start | bytes 388
  19.8 8.0 %copy-start.16 = (f32[64]{0:T(128)S(1)}, f32[64]{0:T(128)}, u32[]{:S(2)}) copy-start(f32[64]{0:T(128)} %param.26) | copy-start | bytes 772
  19.8 8.1 %copy-start.12 = (f32[64]{0:T(128)S(1)}, f32[64]{0:T(128)}, u32[]{:S(2)}) copy-start(f32[64]{0:T(128)} %param.25) | copy-start | bytes 772
  19.8 8.2 %copy-start.5 = (bf16[64,64]{1,0:T(8,128)(2,1)S(1)}, bf16[64,64]{1,0:T(8,128)(2,1)}, u32[]{:S(2)}) copy-start(bf16[64,64]{1,0:T(8,128)(2,1)} %param.24) | copy-start | bytes 24580
  19.8 8.4 %copy-start.3 = (bf16[64,4096]{1,0:T(8,128)(2,1)S(1)}, bf16[64,4096]{1,0:T(8,128)(2,1)}, u32[]{:S(2)}) copy-start(bf16[64,4096]{1,0:T(8,128)(2,1)} %param.20) | copy-start | bytes 1572868
  23.8 104.2 %all-to-all-start = ((bf16[2,64,64,128]{3,2,0,1:T(8,128)(2,1)}), bf16[2,64,64,128]{3,2,0,1:T(8,128)(2,1)}, u32[]{:S(2)}, u32[]{:S(2)}) async-start(bf16[2,64,64,128]{3,2,0,1:T(8,128)(2,1)} %copy.105), calls=%async_computation | async-start | bytes 4194304 | tf_op jit(solution)/shard_map/all_to_all | solution.py:75
  27.2 2.2 copy-start.6
  27.3 2.1 copy-start.9
  27.3 2.3 copy-start.17
  34.0 3.9 copy-start.18
  143.9 32.4 %copy-start.8 = (f32[4096]{0:T(1024)S(1)}, f32[4096]{0:T(1024)}, u32[]{:S(2)}) copy-start(f32[4096]{0:T(1024)} %param.28) | copy-start | bytes 49156
  143.9 30.9 %all-to-all-start.2 = ((bf16[32,64,128]{2,1,0:T(8,128)(2,1)}), bf16[32,64,128]{2,1,0:T(8,128)(2,1)S(1)}, u32[]{:S(2)}, u32[]{:S(2)}) async-start(bf16[32,64,128]{2,1,0:T(8,128)(2,1)} %all_to_all.45), calls=%async_computation.2 | async-start | bytes 1048576 | tf_op jit(solution)/shard_map/all_to_all | solution.py:93
  163.9 12.7 %copy-start.4 = (bf16[64,2048]{1,0:T(8,128)(2,1)S(1)}, bf16[64,2048]{1,0:T(8,128)(2,1)}, u32[]{:S(2)}) copy-start(bf16[64,2048]{1,0:T(8,128)(2,1)} %param.31) | copy-start | bytes 786436
  176.5 9.1 %copy-start.2 = (bf16[64,4096]{1,0:T(8,128)(2,1)}, bf16[64,4096]{1,0:T(8,128)(2,1)S(1)}, u32[]{:S(2)}) copy-start(bf16[64,4096]{1,0:T(8,128)(2,1)S(1)} %multiply_convert_fusion.3) | copy-start | bytes 1572868
  176.5 9.1 %copy-start.10 = (f32[2048]{0:T(1024)S(1)}, f32[2048]{0:T(1024)}, u32[]{:S(2)}) copy-start(f32[2048]{0:T(1024)} %param.33) | copy-start | bytes 24580
  194.4 98.4 %copy-start.14 = (bf16[1,2048,384]{2,1,0:T(8,128)(2,1)S(1)}, bf16[1,2048,384]{2,1,0:T(8,128)(2,1)}, u32[]{:S(2)}) copy-start(bf16[1,2048,384]{2,1,0:T(8,128)(2,1)} %param.37) | copy-start | bytes 4718596
  290.8 2.0 copy-start.1
  292.8 3.6 copy-start.15
  304.1 4.4 %copy-start.7 = (s32[64,10]{0,1:T(8,128)S(1)}, s32[64,10]{0,1:T(8,128)}, u32[]{:S(2)}) copy-start(s32[64,10]{0,1:T(8,128)} %param.35) | copy-start | bytes 7684
  304.1 97.7 %all-to-all-start.4 = ((bf16[32,32,2048]{2,1,0:T(8,128)(2,1)}), bf16[32,32,2048]{2,1,0:T(8,128)(2,1)}, u32[]{:S(2)}, u32[]{:S(2)}) async-start(bf16[32,32,2048]{2,1,0:T(8,128)(2,1)} %bitcast.88), calls=%async_computation.4 | async-start | bytes 8388608 | tf_op jit(solution)/shard_map/all_to_all | solution.py:143
Sparse Core Ops, SparseCore 0:
  10.8 151.8 all-gather.1
where the time goes:
time: 431 us; the launch traced here: 430 us
  blocking collectives  180 us (42%)
  waiting for transfers between devices  109 us (25%)
  local copies, waits for them, and re-layouts  55 us (13%)
  starting transfers between devices  30.1 us (7%)
  matrix products  26.2 us (6%)
  other arithmetic  15.2 us (4%)
  between operations  14.5 us (3%)
    all_to_all x1, blocking collectives, local(): lax.all_to_all(send_rows, 'wide', split_axis=0, concat_axis=0, tiled=True)  96.4 us
    all_to_all x1, waiting for transfers between devices, local(): lax.all_to_all(outputs, 'wide', split_axis=0, concat_axis=0, tiled=True)  93.2 us
    all_gather x1, blocking collectives, local(): c_all = lax.all_gather(ssd_c, 'wide', axis=0, tiled=True)  84.1 us
    all_to_all x1, starting transfers between devices, local(): lax.all_to_all(carried_head.reshape(tokens_all, per_dev * head_dim), 'wid...  15.3 us
    gather x2, local copies, waits for them, and re-layouts, local(): jnp.take(returned.reshape(devices * capacity, width), position, axis=0)  15.1 us
    all_to_all x1, waiting for transfers between devices, local(): lax.all_to_all(carried_head.reshape(tokens_all, per_dev * head_dim), 'wid...  10.9 us
    dot_general x1, matrix products, local(): jnp.dot(ssd_out, lax.all_gather(w_out, 'wide', axis=0, tiled=True), prefe...  9.07 us
  transfers between devices with their start and end apart: 5, of which 3 were waited for; matrix products, arithmetic and copies ran while one was open for 9% of the time, Pallas kernels for 0%

commit v1 on v0

--- a/solution.py
+++ b/solution.py
@@ -90,12 +90,20 @@
     head_raw = lax.all_to_all(dt_raw, "wide", split_axis=1, concat_axis=0, tiled=True)
     step_size, cumulative = head_steps(head_raw, bias_part, rate_part, requests)
     carried_head = state_terms(c_all.reshape(requests, SEQ, state_size), cumulative, start_state)
-    carried = lax.all_to_all(
-        carried_head.reshape(tokens_all, per_dev * head_dim),
-        "wide",
-        split_axis=0,
-        concat_axis=1,
-        tiled=True,
+    carried = jnp.concatenate(
+        lax.all_to_all(
+            jnp.stack(
+                jnp.split(
+                    carried_head.reshape(tokens_all, per_dev * head_dim),
+                    lax.axis_size("wide"),
+                    axis=0,
+                )
+            ),
+            "wide",
+            0,
+            0,
+        ),
+        axis=1,
     )
     mixed = intra.astype(jnp.float32) + carried.astype(jnp.float32)
     gated = mixed * jax.nn.silu(ssd_z.astype(jnp.float32))

time: 431 us -> 454 us (1.053)
  local copies, waits for them, and re-layouts: 55 us -> 77.4 us
    unnamed x40 -> x81, local copies, waits for them, and re-layouts: 6.61 us -> 26.4 us
    another operation x0 -> x33, local copies, waits for them, and re-layouts: none -> 5.94 us  [local(): jnp.stack(jnp.split(carried_head.reshape(tokens_all, per_dev * head_dim),...]
  transfers between devices with their start and end apart: 5 -> 5, of which waited for: 3 -> 3; matrix products, arithmetic and copies ran while one was open for 9% -> 14% of each run, Pallas kernels for 0% -> 0%
where the time goes in v1:
time: 454 us; the launch traced here: 453 us
  blocking collectives  180 us (40%)
  waiting for transfers between devices  109 us (24%)
  local copies, waits for them, and re-layouts  77.4 us (17%)
  starting transfers between devices  29.9 us (7%)
  matrix products  26.2 us (6%)
  other arithmetic  15.2 us (3%)
  between operations  14.8 us (3%)
    all_to_all x1, blocking collectives, local(): lax.all_to_all(send_rows, 'wide', split_axis=0, concat_axis=0, tiled=True)  96.4 us
    all_to_all x1, waiting for transfers between devices, local(): lax.all_to_all(outputs, 'wide', split_axis=0, concat_axis=0, tiled=True)  93.2 us
    all_gather x1, blocking collectives, local(): c_all = lax.all_gather(ssd_c, 'wide', axis=0, tiled=True)  84.1 us
    unnamed x81, local copies, waits for them, and re-layouts  26.4 us
    all_to_all x1, starting transfers between devices, local(): lax.all_to_all(jnp.stack(jnp.split(carried_head.reshape(tokens_all, per_d...  15.2 us
    gather x2, local copies, waits for them, and re-layouts, local(): jnp.take(returned.reshape(devices * capacity, width), position, axis=0)  15 us
    all_to_all x1, waiting for transfers between devices, local(): lax.all_to_all(jnp.stack(jnp.split(carried_head.reshape(tokens_all, per_d...  10.9 us
  transfers between devices with their start and end apart: 5, of which 3 were waited for; matrix products, arithmetic and copies ran while one was open for 14% of the time, Pallas kernels for 0%

profile of v1, /device:TPU:0, one launch (start us, length us, event | category | flops | bytes accessed | tf_op | source)
XLA Modules:
  0.0 452.6 jit_solution(13622627589758747923)
XLA Ops:
  9.3 7.3 %all-to-all-start.1 = ((bf16[64,32,2]{0,2,1:T(2,128)(2,1)}), bf16[64,32,2]{0,2,1:T(2,128)(2,1)S(1)}, u32[]{:S(2)}, u32[]{:S(2)}) async-start(bf16[64,32,2]{0,2,1:T(2,128)(2,1)} %bitcast.14), calls=%async_computation.1 | async-start | bytes 32768 | tf_op jit(solution)/shard_map/all_to_all | solution.py:90
  16.7 3.1 copy.229
  19.8 3.9 all-to-all-done.1
  23.8 3.5 all-to-all-start
  31.5 2.5 copy.228
  38.0 84.1 %all_gather.6 = bf16[2048,128]{1,0:T(8,128)(2,1)S(1)} all-gather(bf16[64,128]{1,0:T(8,128)(2,1)S(1)} %copy-done.11), channel_id=1, replica_groups=mesh['group'=1,'wide'=32] {'wide'}, dimensions={0}, use_global_device_ids=true | all-gather | bytes 540672 | tf_op jit(solution)/shard_map/all_gather | solution.py:89
  123.7 2.4 reduce-window_exponential_fusion
  127.9 3.2 copy.231
  131.1 3.7 gather_fusion
  134.9 3.7 fusion
  166.6 15.2 %all-to-all-start.2 = ((bf16[32,64,128]{2,1,0:T(8,128)(2,1)}), bf16[32,64,128]{2,1,0:T(8,128)(2,1)S(1)}, u32[]{:S(2)}, u32[]{:S(2)}) async-start(bf16[32,64,128]{2,1,0:T(8,128)(2,1)} %constant_dynamic-update-slice_fusion), calls=%async_computation.2 | async-start | bytes 1048576 | tf_op jit(solution)/shard_map/all_to_all | solution.py:94
  182.2 4.1 scatter_custom_fusion
  186.5 10.9 %all-to-all-done.2 = bf16[32,64,128]{2,1,0:T(8,128)(2,1)S(1)} async-done(((bf16[32,64,128]{2,1,0:T(8,128)(2,1)}), bf16[32,64,128]{2,1,0:T(8,128)(2,1)S(1)}, u32[]{:S(2)}, u32[]{:S(2)}) %all-to-all-start.2) | async-done | bytes 524320 | tf_op jit(solution)/shard_map/all_to_all | solution.py:94
  199.3 9.1 %multiply_reduce_fusion.2 = (f32[64]{0:T(128)S(1)}, f32[64,2048]{1,0:T(8,128)S(1)}) fusion(bf16[64,4096]{1,0:T(8,128)(2,1)S(1)} %multiply_convert_fusion.3, bf16[4096,2048]{1,0:T(8,128)(2,1)} %all-gather.2.cloned.1.call-done, bf16[64,2048]{1,0:T(8,128)(2,1)S(1)} %copy-done.5), kind=kOutput, calls=%fused_computation.42 | convolution fusion | flops 1074266112 | bytes 18088192 | tf_op jit(solution)/shard_map/dot_general | solution.py:114
  208.5 6.0 %gather_fusion.1 = bf16[1024,2048]{1,0:T(8,128)(2,1)} fusion(bf16[64,2048]{1,0:T(8,128)(2,1)S(1)} %multiply_convert_fusion.4, s32[1024]{0:T(1024)S(1)} %fusion.38), kind=kCustom, calls=%fused_computation.1 | custom fusion | bytes 8392704 | tf_op jit(solution)/shard_map/jit(_take)/gather | solution.py:144
  214.5 2.6 select_select_fusion
  217.0 96.4 %all_to_all.46 = bf16[32,32,2048]{2,1,0:T(8,128)(2,1)S(1)} all-to-all(bf16[32,32,2048]{2,1,0:T(8,128)(2,1)S(1)} %select_select_fusion), channel_id=1, replica_groups=mesh['group'=1,'wide'=32] {'wide'}, dimensions={0} | all-to-all | bytes 8388608 | tf_op jit(solution)/shard_map/all_to_all | solution.py:148
  315.4 3.6 fusion.8
  319.0 7.8 %convolution_convert_fusion = bf16[1024,2048]{1,0:T(8,128)(2,1)} fusion(bf16[1,384,2048]{2,1,0:T(8,128)(2,1)S(1)} %copy-done, f32[1024,384]{1,0:T(8,128)} %fusion.8, bf16[1024,2048]{1,0:T(8,128)(2,1)} %bitcast.90, bf16[1,2048,384]{2,1,0:T(8,128)(2,1)S(1)} %copy-done.20), kind=kOutput, calls=%fused_computation.6 | convolution fusion | flops 3225681920 | bytes 13107200 | tf_op jit(solution)/shard_map/dot_general | solution.py:33
  326.8 3.8 all-to-all-start.4
  331.1 93.2 %all-to-all-done.4 = bf16[32,32,2048]{2,1,0:T(8,128)(2,1)} async-done(((bf16[32,32,2048]{2,1,0:T(8,128)(2,1)}), bf16[32,32,2048]{2,1,0:T(8,128)(2,1)}, u32[]{:S(2)}, u32[]{:S(2)}) %all-to-all-start.4) | async-done | bytes 4194336 | tf_op jit(solution)/shard_map/all_to_all | solution.py:151
  424.3 9.7 %gather_fusion.2 = bf16[640,2048]{1,0:T(8,128)(2,1)} fusion(bf16[1024,2048]{1,0:T(8,128)(2,1)} %bitcast.24, s32[1024]{0:T(1024)S(1)} %pad_clamp_fusion), kind=kCustom, calls=%fused_computation.2 | custom fusion | bytes 5245440 | tf_op jit(solution)/shard_map/jit(_take)/gather | solution.py:152
  434.0 5.4 %gather.20 = bf16[64,10,2048]{2,1,0:T(8,128)(2,1)} reshape(bf16[640,2048]{1,0:T(8,128)(2,1)} %gather_fusion.2) | data formatting | bytes 5242880 | tf_op jit(solution)/shard_map/jit(_take)/gather | solution.py:152
  439.3 6.4 %multiply_reduce_fusion = bf16[64,2048]{1,0:T(8,128)(2,1)} fusion(f32[64,10]{1,0:T(8,128)S(1)} %copy.276, bf16[64,10,2048]{2,1,0:T(8,128)(2,1)} %gather.20, pred[64,10]{1,0:T(8,128)(4,1)S(1)} %copy.274), kind=kLoop, calls=%fused_computation.4 | loop fusion | flops 5111808 | bytes 2886784 | tf_op jit(solution)/shard_map/reduce_sum | solution.py:155
  (205 shorter events, 46.3 us)
Async XLA Ops:
  7.2 311.8 %copy-start = (bf16[1,384,2048]{2,1,0:T(8,128)(2,1)S(1)}, bf16[1,384,2048]{2,1,0:T(8,128)(2,1)}, u32[]{:S(2)}) copy-start(bf16[1,384,2048]{2,1,0:T(8,128)(2,1)} %param.39) | copy-start | bytes 4718596
  7.2 192.1 %all-gather.2.cloned.1.call-start = ((), (), s32[]{:S(2)}) async-start(), calls=%async_computation.5 | async-start | bytes 17301504 | tf_op jit(solution)/shard_map/all_gather | solution.py:116
  9.3 14.4 %all-to-all-start.1 = ((bf16[64,32,2]{0,2,1:T(2,128)(2,1)}), bf16[64,32,2]{0,2,1:T(2,128)(2,1)S(1)}, u32[]{:S(2)}, u32[]{:S(2)}) async-start(bf16[64,32,2]{0,2,1:T(2,128)(2,1)} %bitcast.14), calls=%async_computation.1 | async-start | bytes 32768 | tf_op jit(solution)/shard_map/all_to_all | solution.py:90
  19.8 7.5 %copy-start.16 = (s32[64,10]{0,1:T(8,128)S(1)}, s32[64,10]{0,1:T(8,128)}, u32[]{:S(2)}) copy-start(s32[64,10]{0,1:T(8,128)} %param.34) | copy-start | bytes 7684
  19.8 7.5 %copy-start.18 = (s32[32]{0:T(128)S(1)}, s32[32]{0:T(128)}, u32[]{:S(2)}) copy-start(s32[32]{0:T(128)} %param.36) | copy-start | bytes 388
  19.8 8.0 %copy-start.21 = (f32[64]{0:T(128)S(1)}, f32[64]{0:T(128)}, u32[]{:S(2)}) copy-start(f32[64]{0:T(128)} %param.26) | copy-start | bytes 772
  19.8 8.1 %copy-start.17 = (f32[64]{0:T(128)S(1)}, f32[64]{0:T(128)}, u32[]{:S(2)}) copy-start(f32[64]{0:T(128)} %param.25) | copy-start | bytes 772
  19.8 8.2 %copy-start.6 = (bf16[64,64]{1,0:T(8,128)(2,1)S(1)}, bf16[64,64]{1,0:T(8,128)(2,1)}, u32[]{:S(2)}) copy-start(bf16[64,64]{1,0:T(8,128)(2,1)} %param.24) | copy-start | bytes 24580
  19.8 8.4 %copy-start.4 = (bf16[64,4096]{1,0:T(8,128)(2,1)S(1)}, bf16[64,4096]{1,0:T(8,128)(2,1)}, u32[]{:S(2)}) copy-start(bf16[64,4096]{1,0:T(8,128)(2,1)} %param.20) | copy-start | bytes 1572868
  23.8 104.2 %all-to-all-start = ((bf16[2,64,64,128]{3,2,0,1:T(8,128)(2,1)}), bf16[2,64,64,128]{3,2,0,1:T(8,128)(2,1)}, u32[]{:S(2)}, u32[]{:S(2)}) async-start(bf16[2,64,64,128]{3,2,0,1:T(8,128)(2,1)} %copy.229), calls=%async_computation | async-start | bytes 4194304 | tf_op jit(solution)/shard_map/all_to_all | solution.py:75
  34.0 3.9 copy-start.23
  143.9 11.2 %copy-start.7 = (bf16[1,64,128]{2,1,0:T(8,128)(2,1)S(1)}, bf16[1,64,128]{2,1,0:T(8,128)(2,1)}, u32[]{:S(2)}) copy-start(bf16[1,64,128]{2,1,0:T(8,128)(2,1)} %stack.112) | copy-start | bytes 49156
  143.9 11.8 %copy-start.8 = (bf16[1,64,128]{2,1,0:T(8,128)(2,1)S(1)}, bf16[1,64,128]{2,1,0:T(8,128)(2,1)}, u32[]{:S(2)}) copy-start(bf16[1,64,128]{2,1,0:T(8,128)(2,1)} %stack.113) | copy-start | bytes 49156
  144.6 11.7 %copy-start.9 = (bf16[1,64,128]{2,1,0:T(8,128)(2,1)S(1)}, bf16[1,64,128]{2,1,0:T(8,128)(2,1)}, u32[]{:S(2)}) copy-start(bf16[1,64,128]{2,1,0:T(8,128)(2,1)} %stack.114) | copy-start | bytes 49156
  145.4 12.1 %copy-start.10 = (bf16[1,64,128]{2,1,0:T(8,128)(2,1)S(1)}, bf16[1,64,128]{2,1,0:T(8,128)(2,1)}, u32[]{:S(2)}) copy-start(bf16[1,64,128]{2,1,0:T(8,128)(2,1)} %stack.116) | copy-start | bytes 49156
  166.6 32.4 %copy-start.13 = (f32[4096]{0:T(1024)S(1)}, f32[4096]{0:T(1024)}, u32[]{:S(2)}) copy-start(f32[4096]{0:T(1024)} %param.28) | copy-start | bytes 49156
  166.6 30.8 %all-to-all-start.2 = ((bf16[32,64,128]{2,1,0:T(8,128)(2,1)}), bf16[32,64,128]{2,1,0:T(8,128)(2,1)S(1)}, u32[]{:S(2)}, u32[]{:S(2)}) async-start(bf16[32,64,128]{2,1,0:T(8,128)(2,1)} %constant_dynamic-update-slice_fusion), calls=%async_computation.2 | async-start | bytes 1048576 | tf_op jit(solution)/shard_map/all_to_all | solution.py:94
  186.5 12.7 %copy-start.5 = (bf16[64,2048]{1,0:T(8,128)(2,1)S(1)}, bf16[64,2048]{1,0:T(8,128)(2,1)}, u32[]{:S(2)}) copy-start(bf16[64,2048]{1,0:T(8,128)(2,1)} %param.31) | copy-start | bytes 786436
  199.2 9.1 %copy-start.2 = (bf16[64,4096]{1,0:T(8,128)(2,1)}, bf16[64,4096]{1,0:T(8,128)(2,1)S(1)}, u32[]{:S(2)}) copy-start(bf16[64,4096]{1,0:T(8,128)(2,1)S(1)} %multiply_convert_fusion.3) | copy-start | bytes 1572868
  199.2 9.1 %copy-start.15 = (f32[2048]{0:T(1024)S(1)}, f32[2048]{0:T(1024)}, u32[]{:S(2)}) copy-start(f32[2048]{0:T(1024)} %param.33) | copy-start | bytes 24580
  217.0 98.4 %copy-start.19 = (bf16[1,2048,384]{2,1,0:T(8,128)(2,1)S(1)}, bf16[1,2048,384]{2,1,0:T(8,128)(2,1)}, u32[]{:S(2)}) copy-start(bf16[1,2048,384]{2,1,0:T(8,128)(2,1)} %param.37) | copy-start | bytes 4718596
  315.4 3.6 copy-start.20
  326.8 4.1 copy-start.12
  326.8 97.5 %all-to-all-start.4 = ((bf16[32,32,2048]{2,1,0:T(8,128)(2,1)}), bf16[32,32,2048]{2,1,0:T(8,128)(2,1)}, u32[]{:S(2)}, u32[]{:S(2)}) async-start(bf16[32,32,2048]{2,1,0:T(8,128)(2,1)} %bitcast.88), calls=%async_computation.4 | async-start | bytes 8388608 | tf_op jit(solution)/shard_map/all_to_all | solution.py:151
  (5 other events, 9.5 us)
Sparse Core Ops, SparseCore 0:
  10.8 151.8 all-gather.1
